TPU v7x, 32 devices: a whole 2x2x4 slice. The times are simulated.
32 devices in a mesh: groups: 2 (over x), img: 16 (over z, y, core).
Axes of the slice: x: 2, y: 2, z: 4, core: 2. Of those that a mesh axis runs over, the one named last changes fastest.
Arguments:
- tokens: bfloat16 [64, 128, 768], P(('groups', 'img')), parts along dimension 0, may hold values from -6 to 6
- partners: int32 [64, 8], P(('groups', 'img')), parts along dimension 0, may hold values from 0 to 31, as said below
- counts: int32 [64], P(('groups', 'img')), parts along dimension 0, may hold values from 4 to 8, as said below
- gain_query: float32 [768], replicated, may hold values from 0.5 to 12
- gain_memory: float32 [768], replicated, may hold values from 0.25 to 1.75
- w_query: bfloat16 [768, 768], replicated, may hold values from -0.21875 to 0.21875
- w_key: bfloat16 [768, 768], replicated, may hold values from -0.21875 to 0.21875
- w_value: bfloat16 [768, 768], replicated, may hold values from -0.21875 to 0.21875
- w_out: bfloat16 [768, 768], replicated, may hold values from -0.21875 to 0.21875
Outputs:
- mixed: bfloat16 [64, 128, 768], P(('groups', 'img')), parts along dimension 0
There are 2 independent parts, one for each index of `groups`. A program takes and returns all parts, laid end to end along the dimension named above; an argument that names none is the same for every part. Nothing has to cross between parts.
Inputs may be any that keep to these rules, and one draw needn't show every extreme that they name: No image is its own partner. Over the first counts[a] partners of all images a of one device (image i belongs to device i // 2), at most 1 lie with any one device, and every device reaches 1 with some device. `counts`: every device owns an image with 8 pairs.
All inputs are finite; a program needn't handle non-finite values.
Results may differ from a plain program's by a relative error of at most 0.0067.
Values may be sent and summed in bfloat16 or wider, within the bound.
A program may use at most 128 MiB of HBM per device.

v0:
```python
import jax
import jax.numpy as jnp
from jax import lax
from jax.sharding import PartitionSpec as P

HEADS = 12
HEAD_DIM = 64


def normalize(rows, gain):
    rows = rows.astype(jnp.float32)
    center = rows - jnp.mean(rows, axis=-1, keepdims=True)
    spread = jnp.mean(center * center, axis=-1, keepdims=True)
    return center * lax.rsqrt(spread + 1e-06) * gain


def slot_table(partner_rows, count_rows, own_count, peer_count):
    width = partner_rows.shape[1]
    live = (jnp.arange(width, dtype=jnp.int32)[None, :] < count_rows[:, None]).reshape(-1)
    owner = (partner_rows // own_count).reshape(-1)
    onehot = (
        (owner[:, None] == jnp.arange(peer_count, dtype=jnp.int32)[None, :]) & live[:, None]
    ).astype(jnp.int32)
    before = jnp.cumsum(onehot, axis=0) - onehot
    slot = jnp.sum(before * onehot, axis=1)
    return (owner, slot, live)


def shards(tokens, partners, counts, gain_query, gain_memory, w_query, w_key, w_value, w_out):
    own_count, tok_rows, width = tokens.shape
    listed = partners.shape[1]
    peer_count = lax.axis_size("img")
    slot_cap = (own_count * listed + peer_count - 1) // peer_count
    first_image = lax.axis_index("img") * own_count
    rows = tokens.reshape(own_count * tok_rows, width)
    normed_query = normalize(rows, gain_query).astype(jnp.bfloat16)
    normed_memory = normalize(rows, gain_memory).astype(jnp.bfloat16)
    queries = jnp.dot(normed_query, w_query, preferred_element_type=jnp.float32).astype(
        jnp.bfloat16
    )
    queries = queries.reshape(own_count, tok_rows, HEADS, HEAD_DIM)
    my_owner, my_slot, my_live = slot_table(partners, counts, own_count, peer_count)
    target = jnp.where(my_live, my_owner, peer_count)
    request = (
        jnp.full((peer_count, slot_cap), -1, jnp.int32)
        .at[target, my_slot]
        .set(partners.reshape(-1), mode="drop")
    )
    wanted = lax.all_to_all(request, "img", split_axis=0, concat_axis=0, tiled=True)
    used = wanted >= 0
    local_index = jnp.clip(wanted - first_image, 0, own_count - 1)
    pick = jnp.clip(my_owner, 0, peer_count - 1) * slot_cap + jnp.clip(my_slot, 0, slot_cap - 1)
    picked = normed_memory.reshape(own_count, tok_rows, width)[local_index]
    got_memory = lax.all_to_all(
        jnp.where(used[:, :, None, None], picked, jnp.zeros_like(picked)),
        "img",
        split_axis=0,
        concat_axis=0,
        tiled=True,
    )
    pair_memory = got_memory.reshape(peer_count * slot_cap, tok_rows, width)[pick].reshape(
        -1, width
    )
    pair_keys = jnp.dot(pair_memory, w_key, preferred_element_type=jnp.float32).astype(jnp.bfloat16)
    pair_values = jnp.dot(pair_memory, w_value, preferred_element_type=jnp.float32).astype(
        jnp.bfloat16
    )
    pair_keys = pair_keys.reshape(own_count, listed, tok_rows, HEADS, HEAD_DIM)
    pair_values = pair_values.reshape(own_count, listed, tok_rows, HEADS, HEAD_DIM)
    scale = 1.0 / HEAD_DIM**0.5

    def one_image(item):
        query_rows, key_rows, value_rows, count = item
        scores = (
            jnp.einsum("qhd,kjhd->hkqj", query_rows, key_rows, preferred_element_type=jnp.float32)
            * scale
        )
        probs = jax.nn.softmax(scores, axis=-1).astype(jnp.bfloat16)
        pair_context = jnp.einsum(
            "hkqj,kjhd->kqhd", probs, value_rows, preferred_element_type=jnp.float32
        )
        live = jnp.arange(listed, dtype=jnp.int32) < count
        total = jnp.sum(
            jnp.where(live[:, None, None, None], pair_context, jnp.float32(0.0)), axis=0
        )
        return total.reshape(tok_rows, width) / count.astype(jnp.float32)

    context = lax.map(one_image, (queries, pair_keys, pair_values, counts)).astype(jnp.bfloat16)
    mixed = rows.astype(jnp.float32) + jnp.dot(
        context.reshape(-1, width), w_out, preferred_element_type=jnp.float32
    )
    return mixed.astype(jnp.bfloat16).reshape(own_count, tok_rows, width)


def solution(mesh):
    placed = (
        P(("groups", "img"), None, None),
        P(("groups", "img"), None),
        P(("groups", "img")),
        P(),
        P(),
        P(),
        P(),
        P(),
        P(),
    )
    return jax.shard_map(
        shards,
        mesh=mesh,
        in_specs=placed,
        out_specs=P(("groups", "img"), None, None),
        check_vma=False,
    )
```

profile of v0, /device:TPU:13, one launch (start us, length us, event | category | flops | bytes accessed | tf_op | source)
XLA Modules:
  0.0 160.1 jit_solution(5718504146963567102)
XLA Ops:
  5.0 6.6 %all-to-all-start = ((s32[16,1,1]{2,1,0:T(1,128)}), s32[16,1,1]{2,1,0:T(1,128)S(1)}, u32[]{:S(2)}, u32[]{:S(2)}) async-start(s32[16,1,1]{2,1,0:T(1,128)} %copy.39), calls=%async_computation | async-start | bytes 16384 | tf_op jit(solution)/shard_map/all_to_all | solution.py:49
  11.5 1.1 convert_reduce_fusion
  12.6 1.2 multiply_reduce_fusion
  13.9 1.2 multiply_convert_fusion
  15.6 2.5 %gather_fusion = bf16[16,128,768]{2,1,0:T(8,128)(2,1)} fusion(bf16[2,128,768]{2,1,0:T(8,128)(2,1)S(1)} %multiply_convert_fusion, s32[1024]{0:T(1024)S(1)} %pad_clamp_fusion.1), kind=kCustom, calls=%fused_computation | custom fusion | bytes 6291520 | tf_op jit(solution)/shard_map/gather | solution.py:53
  18.5 3.9 %bitcast_select_fusion = bf16[16,1,128,768]{3,2,1,0:T(8,128)(2,1)} fusion(bf16[16,128,768]{2,1,0:T(8,128)(2,1)} %gather_fusion, pred[16]{0:T(512)(128)(4,1)S(1)} %compare_reduce_fusion), kind=kLoop, calls=%fused_computation.28 | loop fusion | flops 1572864 | bytes 6291472 | tf_op jit(solution)/shard_map/jit(_where)/select_n | solution.py:55
  22.3 7.1 %all-to-all-start.1 = ((bf16[16,1,128,768]{3,2,1,0:T(8,128)(2,1)}), bf16[16,1,128,768]{3,2,1,0:T(8,128)(2,1)}, u32[]{:S(2)}, u32[]{:S(2)}) async-start(bf16[16,1,128,768]{3,2,1,0:T(8,128)(2,1)} %bitcast_select_fusion), calls=%async_computation.1 | async-start | bytes 6291456 | tf_op jit(solution)/shard_map/all_to_all | solution.py:54
  30.5 68.9 %all-to-all-done.1 = bf16[16,1,128,768]{3,2,1,0:T(8,128)(2,1)} async-done(((bf16[16,1,128,768]{3,2,1,0:T(8,128)(2,1)}), bf16[16,1,128,768]{3,2,1,0:T(8,128)(2,1)}, u32[]{:S(2)}, u32[]{:S(2)}) %all-to-all-start.1) | async-done | bytes 3145760 | tf_op jit(solution)/shard_map/all_to_all | solution.py:54
  99.4 4.3 %gather_fusion.1 = bf16[16,128,768]{2,1,0:T(8,128)(2,1)} fusion(bf16[16,128,768]{2,1,0:T(8,128)(2,1)} %bitcast.14, s32[1024]{0:T(1024)S(1)} %pad_clamp_fusion), kind=kCustom, calls=%fused_computation.1 | custom fusion | bytes 6291520 | tf_op jit(solution)/shard_map/gather | solution.py:61
  103.8 6.2 %convolution_convert_fusion.1 = bf16[2048,768]{1,0:T(8,128)(2,1)} fusion(bf16[2048,768]{1,0:T(8,128)(2,1)} %bitcast.100, bf16[768,768]{1,0:T(8,128)(2,1)S(1)} %copy-done), kind=kOutput, calls=%fused_computation.27 | convolution fusion | flops 2417491968 | bytes 7471104 | tf_op jit(solution)/shard_map/dot_general | solution.py:65
  110.0 4.8 %copy.40 = bf16[2048,768]{0,1:T(8,128)(2,1)} copy(bf16[2048,768]{1,0:T(8,128)(2,1)} %convolution_convert_fusion.1) | data formatting | bytes 6291456 | tf_op jit(solution)/shard_map/convert_element_type | solution.py:65
  114.7 4.7 %copy.56 = bf16[96,8,16,128]{3,2,1,0:T(8,128)(2,1)} copy(bf16[96,8,16,128]{3,1,2,0:T(8,128)(2,1)} %bitcast.97) | data formatting | bytes 6291456
  119.5 4.0 %convolution_convert_fusion = bf16[2048,768]{1,0:T(8,128)(2,1)} fusion(bf16[2048,768]{1,0:T(8,128)(2,1)S(1)} %bitcast.101, bf16[768,768]{1,0:T(8,128)(2,1)S(1)} %copy-done.7), kind=kOutput, calls=%fused_computation.26 | convolution fusion | flops 2417491968 | bytes 7471104 | tf_op jit(solution)/shard_map/dot_general | solution.py:64
  123.4 4.8 %copy.41 = bf16[2048,768]{0,1:T(8,128)(2,1)} copy(bf16[2048,768]{1,0:T(8,128)(2,1)} %convolution_convert_fusion) | data formatting | bytes 6291456 | tf_op jit(solution)/shard_map/convert_element_type | solution.py:64
  128.2 4.7 %copy.57 = bf16[96,8,16,128]{3,2,1,0:T(8,128)(2,1)} copy(bf16[96,8,16,128]{3,1,2,0:T(8,128)(2,1)} %bitcast.98) | data formatting | bytes 6291456
  132.9 24.7 %while.10 = (s32[]{:T(128)}, bf16[2,128,768]{2,1,0:T(8,128)(2,1)S(1)}, s32[2]{0:T(128)S(1)}, bf16[2,8,128,12,64]{2,1,0,4,3:T(8,128)(2,1)}, bf16[2,8,128,12,64]{2...) while((s32[]{:T(128)}, bf16[2,128,768]{2,1,0:T(8,128)(2,1)S(1)}, s32[2]{0:T(128)S(1)}, ...), condition=%wide.region_9.10_spmd, body=%wide.region_5.9_spmd.sunk | while | flops 413761664 | bytes 36667524 | solution.py:88
  132.9 2.2 %constant_dynamic-slice_fusion.3 = (bf16[1,8,128,12,64]{2,1,0,4,3:T(8,128)(2,1)S(1)}, bf16[1,8,128,12,64]{2,1,0,4,3:T(8,128)(2,1)S(1)}) fusion(bf16[2,8,128,12,64]{2,1,0,4,3:T(8,128)(2,1)} %get-tuple-element.155, s32[]{:T(128)} %get-tuple-element.144, bf16[2,8,128,12,64]{2,1,0,4,3:T(8,128)(2,1)} %get-tuple-element.154), kind=kLoop, calls=%fused_computation.22.clone.1 | loop fusion | bytes 6291460 | tf_op jit(solution)/shard_map/while/body/jit(dynamic_index_in_dim)/dynamic_slice | solution.py:88
  135.0 1.1 fusion.46
  136.1 5.9 %fusion.47 = (f32[12,8,128]{2,1,0:T(8,128)S(1)}, f32[12,8,128,128]{2,3,1,0:T(8,128)S(1)}) fusion(f32[12,8,128,128]{3,2,1,0:T(8,128)S(1)} %fusion.46), kind=kOutput, calls=%fused_computation.70.clone.1 | output fusion | flops 6291583 | bytes 12632064 | tf_op jit(solution)/shard_map/while/body/eval_jaxpr/sub | solution.py:78
  143.3 1.0 select_reduce_fusion.3
  145.2 2.2 %constant_dynamic-slice_fusion.3 = (bf16[1,8,128,12,64]{2,1,0,4,3:T(8,128)(2,1)S(1)}, bf16[1,8,128,12,64]{2,1,0,4,3:T(8,128)(2,1)S(1)}) fusion(bf16[2,8,128,12,64]{2,1,0,4,3:T(8,128)(2,1)} %get-tuple-element.155, s32[]{:T(128)} %get-tuple-element.144, bf16[2,8,128,12,64]{2,1,0,4,3:T(8,128)(2,1)} %get-tuple-element.154), kind=kLoop, calls=%fused_computation.22.clone.1 | loop fusion | bytes 6291460 | tf_op jit(solution)/shard_map/while/body/jit(dynamic_index_in_dim)/dynamic_slice | solution.py:88
  147.4 1.1 fusion.46
  148.5 5.9 %fusion.47 = (f32[12,8,128]{2,1,0:T(8,128)S(1)}, f32[12,8,128,128]{2,3,1,0:T(8,128)S(1)}) fusion(f32[12,8,128,128]{3,2,1,0:T(8,128)S(1)} %fusion.46), kind=kOutput, calls=%fused_computation.70.clone.1 | output fusion | flops 6291583 | bytes 12632064 | tf_op jit(solution)/shard_map/while/body/eval_jaxpr/sub | solution.py:78
  157.6 2.5 %fusion.16 = bf16[256,768]{1,0:T(8,128)(2,1)} fusion(bf16[256,768]{1,0:T(8,128)(2,1)S(1)} %bitcast.102, bf16[768,768]{1,0:T(8,128)(2,1)} %param.19, bf16[256,768]{1,0:T(8,128)(2,1)S(1)} %bitcast.99), kind=kOutput, calls=%fused_computation.30 | convolution fusion | flops 302579712 | bytes 2359296 | tf_op jit(solution)/shard_map/dot_general | solution.py:89
  (54 shorter events, 10.8 us)
Async XLA Ops:
  0.0 103.8 %copy-start = (bf16[768,768]{1,0:T(8,128)(2,1)S(1)}, bf16[768,768]{1,0:T(8,128)(2,1)}, u32[]{:S(2)}) copy-start(bf16[768,768]{1,0:T(8,128)(2,1)} %param.18) | copy-start | bytes 3538948
  5.0 10.3 %all-to-all-start = ((s32[16,1,1]{2,1,0:T(1,128)}), s32[16,1,1]{2,1,0:T(1,128)S(1)}, u32[]{:S(2)}, u32[]{:S(2)}) async-start(s32[16,1,1]{2,1,0:T(1,128)} %copy.39), calls=%async_computation | async-start | bytes 16384 | tf_op jit(solution)/shard_map/all_to_all | solution.py:49
  22.3 7.1 %copy-start.1 = (bf16[2,128,768]{2,1,0:T(8,128)(2,1)S(1)}, bf16[2,128,768]{2,1,0:T(8,128)(2,1)}, u32[]{:S(2)}) copy-start(bf16[2,128,768]{2,1,0:T(8,128)(2,1)} %param.11) | copy-start | bytes 1179652
  22.3 7.1 %copy-start.5 = (f32[768]{0:T(1024)S(1)}, f32[768]{0:T(1024)}, u32[]{:S(2)}) copy-start(f32[768]{0:T(1024)} %param.14) | copy-start | bytes 9220
  22.3 7.3 %copy-start.3 = (bf16[768,768]{1,0:T(8,128)(2,1)S(1)}, bf16[768,768]{1,0:T(8,128)(2,1)}, u32[]{:S(2)}) copy-start(bf16[768,768]{1,0:T(8,128)(2,1)} %param.16) | copy-start | bytes 3538948
  22.3 77.1 %all-to-all-start.1 = ((bf16[16,1,128,768]{3,2,1,0:T(8,128)(2,1)}), bf16[16,1,128,768]{3,2,1,0:T(8,128)(2,1)}, u32[]{:S(2)}, u32[]{:S(2)}) async-start(bf16[16,1,128,768]{3,2,1,0:T(8,128)(2,1)} %bitcast_select_fusion), calls=%async_computation.1 | async-start | bytes 6291456 | tf_op jit(solution)/shard_map/all_to_all | solution.py:54
  114.7 4.7 %copy-start.2 = (bf16[16,128,768]{2,1,0:T(8,128)(2,1)S(1)}, bf16[16,128,768]{2,1,0:T(8,128)(2,1)}, u32[]{:S(2)}) copy-start(bf16[16,128,768]{2,1,0:T(8,128)(2,1)} %gather_fusion.1) | copy-start | bytes 9437188
  114.7 4.7 %copy-start.7 = (bf16[768,768]{1,0:T(8,128)(2,1)S(1)}, bf16[768,768]{1,0:T(8,128)(2,1)}, u32[]{:S(2)}) copy-start(bf16[768,768]{1,0:T(8,128)(2,1)} %param.17) | copy-start | bytes 3538948
  128.2 4.7 %copy-start.4 = (bf16[2,128,768]{2,1,0:T(8,128)(2,1)S(1)}, bf16[2,128,768]{2,1,0:T(8,128)(2,1)}, u32[]{:S(2)}) copy-start(bf16[2,128,768]{2,1,0:T(8,128)(2,1)} %custom-call.4) | copy-start | bytes 1179652
  128.2 4.7 %copy-start.6 = (s32[2]{0:T(128)S(1)}, s32[2]{0:T(128)}, u32[]{:S(2)}) copy-start(s32[2]{0:T(128)} %param.13) | copy-start | bytes 28
where the time goes:
time: 161 us; the launch traced here: 160 us
  waiting for transfers between devices  69 us (43%)
  local copies, waits for them, and re-layouts  34.3 us (21%)
  other arithmetic  24.2 us (15%)
  matrix products  17.3 us (11%)
  starting transfers between devices  13.6 us (8%)
    all_to_all x1, waiting for transfers between devices, shards(): lax.all_to_all(jnp.where(used[:, :, None, None], picked, jnp.zeros_like(p...  68.9 us
    sub x2, other arithmetic, one_image(): probs = jax.nn.softmax(scores, axis=-1).astype(jnp.bfloat16)  11.8 us
    unnamed x18, local copies, waits for them, and re-layouts  9.42 us
    all_to_all x1, starting transfers between devices, shards(): lax.all_to_all(jnp.where(used[:, :, None, None], picked, jnp.zeros_like(p...  7.08 us
    all_to_all x1, starting transfers between devices, shards(): lax.all_to_all(request, 'img', split_axis=0, concat_axis=0, tiled=True)  6.55 us
    dot_general x1, matrix products, shards(): jnp.dot(pair_memory, w_value, preferred_element_type=jnp.float32)  6.18 us
    dynamic_slice x4, local copies, waits for them, and re-layouts, shards(): lax.map(one_image, (queries, pair_keys, pair_values, counts))  5.53 us
    convert_element_type x1, local copies, waits for them, and re-layouts, shards(): jnp.dot(pair_memory, w_value, preferred_element_type=jnp.float32)  4.76 us
  transfers between devices with their start and end apart: 2, of which 2 were waited for; matrix products, arithmetic and copies ran while one was open for 3% of the time, Pallas kernels for 0%

commit v1 on v0

--- a/solution.py
+++ b/solution.py
@@ -5,6 +5,17 @@
 
 HEADS = 12
 HEAD_DIM = 64
+
+
+def cut_along(shard, dim, devices):
+    before, after = (shard.shape[:dim], shard.shape[dim + 1 :])
+    return jnp.moveaxis(shard.reshape(*before, devices, -1, *after), dim, 0)
+
+
+def in_order(parts, dim):
+    parts = jnp.moveaxis(parts, 0, dim)
+    dims = parts.shape
+    return parts.reshape(*dims[:dim], dims[dim] * dims[dim + 1], *dims[dim + 2 :])
 
 
 def normalize(rows, gain):
@@ -51,13 +62,15 @@
     local_index = jnp.clip(wanted - first_image, 0, own_count - 1)
     pick = jnp.clip(my_owner, 0, peer_count - 1) * slot_cap + jnp.clip(my_slot, 0, slot_cap - 1)
     picked = normed_memory.reshape(own_count, tok_rows, width)[local_index]
-    got_memory = lax.all_to_all(
-        jnp.where(used[:, :, None, None], picked, jnp.zeros_like(picked)),
-        "img",
-        split_axis=0,
-        concat_axis=0,
-        tiled=True,
-    )
+    shard = jnp.where(used[:, :, None, None], picked, jnp.zeros_like(picked))
+    count_2, index = (lax.axis_size("img"), lax.axis_index("img"))
+    blocks = cut_along(shard, 0, count_2)
+    outs = [blocks[index]]
+    for step in range(1, count_2):
+        sent = blocks[(index + step) % count_2]
+        outs.append(lax.ppermute(sent, "img", [(i, (i + step) % count_2) for i in range(count_2)]))
+    blocks = jnp.stack(outs)[(index - jnp.arange(count_2)) % count_2]
+    got_memory = in_order(blocks, 0)
     pair_memory = got_memory.reshape(peer_count * slot_cap, tok_rows, width)[pick].reshape(
         -1, width
     )

time: 161 us -> 173 us (1.075); the launches traced: 160 us -> 170 us
  waiting for transfers between devices: 69 us -> 50.3 us
  local copies, waits for them, and re-layouts: 34.3 us -> 50.2 us
  starting transfers between devices: 13.6 us -> 20.7 us
  matrix products: 17.3 us -> 22.2 us
    all_to_all x1 -> x0, waiting for transfers between devices: 68.9 us -> none  [shards(): lax.all_to_all(jnp.where(used[:, :, None, None], picked, jnp.zeros_like(p...]
    ppermute x0 -> x15, waiting for transfers between devices: none -> 50.3 us  [shards(): lax.ppermute(sent, 'img', [(i, (i + step) % count_2) for i in range(count...]
    ppermute x0 -> x15, starting transfers between devices: none -> 14.2 us  [shards(): lax.ppermute(sent, 'img', [(i, (i + step) % count_2) for i in range(count...]
    unnamed x18 -> x33, local copies, waits for them, and re-layouts: 9.42 us -> 18.6 us
    all_to_all x1 -> x0, starting transfers between devices: 7.08 us -> none  [shards(): lax.all_to_all(jnp.where(used[:, :, None, None], picked, jnp.zeros_like(p...]
    gather x0 -> x1, local copies, waits for them, and re-layouts: none -> 4.31 us  [shards(): blocks = jnp.stack(outs)[(index - jnp.arange(count_2)) % count_2]]
    div x2, other arithmetic: 0.09 us -> 2.08 us  [one_image(): return total.reshape(tok_rows, width) / count.astype(jnp.float32)]
    dot_general x2, matrix products: 2.17 us -> 4.02 us  [one_image(): jnp.einsum('qhd,kjhd->hkqj', query_rows, key_rows, preferred_element_type...]
  transfers between devices with their start and end apart: 2 -> 16, of which waited for: 2 -> 10; matrix products, arithmetic and copies ran while one was open for 3% -> 10% of each run, Pallas kernels for 0% -> 0%
where the time goes in v1:
time: 173 us; the launch traced here: 170 us
  waiting for transfers between devices  50.3 us (29%)
  local copies, waits for them, and re-layouts  50.2 us (29%)
  other arithmetic  24.8 us (14%)
  matrix products  22.2 us (13%)
  starting transfers between devices  20.7 us (12%)
    ppermute x15, waiting for transfers between devices, shards(): lax.ppermute(sent, 'img', [(i, (i + step) % count_2) for i in range(count...  50.3 us
    unnamed x33, local copies, waits for them, and re-layouts  18.6 us
    ppermute x15, starting transfers between devices, shards(): lax.ppermute(sent, 'img', [(i, (i + step) % count_2) for i in range(count...  14.2 us
    sub x2, other arithmetic, one_image(): probs = jax.nn.softmax(scores, axis=-1).astype(jnp.bfloat16)  11.8 us
    all_to_all x1, starting transfers between devices, shards(): lax.all_to_all(request, 'img', split_axis=0, concat_axis=0, tiled=True)  6.55 us
    dot_general x1, matrix products, shards(): jnp.dot(pair_memory, w_value, preferred_element_type=jnp.float32)  6.18 us
    dynamic_slice x4, local copies, waits for them, and re-layouts, shards(): lax.map(one_image, (queries, pair_keys, pair_values, counts))  4.96 us
    convert_element_type x1, local copies, waits for them, and re-layouts, shards(): jnp.dot(pair_memory, w_value, preferred_element_type=jnp.float32)  4.73 us
  transfers between devices with their start and end apart: 16, of which 10 were waited for; matrix products, arithmetic and copies ran while one was open for 10% of the time, Pallas kernels for 0%

profile of v1, /device:TPU:13, one launch (start us, length us, event | category | flops | bytes accessed | tf_op | source)
XLA Modules:
  0.0 169.8 jit_solution(2842850364807580609)
XLA Ops:
  4.9 6.6 %all-to-all-start = ((s32[16,1,1]{2,1,0:T(1,128)}), s32[16,1,1]{2,1,0:T(1,128)S(1)}, u32[]{:S(2)}, u32[]{:S(2)}) async-start(s32[16,1,1]{2,1,0:T(1,128)} %copy.95), calls=%async_computation | async-start | bytes 16384 | tf_op jit(solution)/shard_map/all_to_all | solution.py:60
  18.8 2.4 %gather_fusion = bf16[16,128,768]{2,1,0:T(8,128)(2,1)} fusion(bf16[2,128,768]{2,1,0:T(8,128)(2,1)S(1)} %multiply_convert_fusion, s32[1024]{0:T(1024)S(1)} %get-tuple-element.107), kind=kCustom, calls=%fused_computation | custom fusion | bytes 6291520 | tf_op jit(solution)/shard_map/gather | solution.py:64
  21.6 2.3 %fusion.42 = bf16[16,1,128,768]{3,2,1,0:T(8,128)(2,1)S(1)} fusion(bf16[16,128,768]{2,1,0:T(8,128)(2,1)} %gather_fusion, pred[16]{0:T(512)(128)(4,1)S(1)} %compare_reduce_fusion), kind=kLoop, calls=%fused_computation.110 | loop fusion | flops 1572864 | bytes 6291472 | tf_op jit(solution)/shard_map/jit(_where)/select_n | solution.py:65
  28.9 2.9 %collective-permute-start.4 = (bf16[1,1,128,768]{3,2,1,0:T(8,128)(2,1)S(1)}, bf16[1,1,128,768]{3,2,1,0:T(8,128)(2,1)S(1)}, u32[]{:S(2)}, u32[]{:S(2)}) collective-permute-start(bf16[1,1,128,768]{3,2,1,0:T(8,128)(2,1)S(1)} %get-tuple-element.95), channel_id=1, source_target_pairs={{0,5},{1,6},{2,7},{3,8},{4,9},{5,10},{6,11},{7,12},{8,13},{9,14},{... | collective-permute-start | bytes 589832 | tf_op jit(solution)/shard_map/ppermute | solution.py:71
  32.5 2.1 %collective-permute-start.5 = (bf16[1,1,128,768]{3,2,1,0:T(8,128)(2,1)S(1)}, bf16[1,1,128,768]{3,2,1,0:T(8,128)(2,1)S(1)}, u32[]{:S(2)}, u32[]{:S(2)}) collective-permute-start(bf16[1,1,128,768]{3,2,1,0:T(8,128)(2,1)S(1)} %get-tuple-element.94), channel_id=1, source_target_pairs={{0,6},{1,7},{2,8},{3,9},{4,10},{5,11},{6,12},{7,13},{8,14},{9,15},... | collective-permute-start | bytes 589832 | tf_op jit(solution)/shard_map/ppermute | solution.py:71
  40.2 4.0 %collective-permute-done.3 = bf16[1,1,128,768]{3,2,1,0:T(8,128)(2,1)S(1)} collective-permute-done((bf16[1,1,128,768]{3,2,1,0:T(8,128)(2,1)S(1)}, bf16[1,1,128,768]{3,2,1,0:T(8,128)(2,1)S(1)}, u32[]{:S(2)}, u32[]{:S(2)}) %collective-permute-start.3) | collective-permute-done | bytes 196640 | tf_op jit(solution)/shard_map/ppermute | solution.py:71
  44.9 27.8 %collective-permute-done.4 = bf16[1,1,128,768]{3,2,1,0:T(8,128)(2,1)S(1)} collective-permute-done((bf16[1,1,128,768]{3,2,1,0:T(8,128)(2,1)S(1)}, bf16[1,1,128,768]{3,2,1,0:T(8,128)(2,1)S(1)}, u32[]{:S(2)}, u32[]{:S(2)}) %collective-permute-start.4) | collective-permute-done | bytes 196640 | tf_op jit(solution)/shard_map/ppermute | solution.py:71
  73.4 3.5 %collective-permute-done.5 = bf16[1,1,128,768]{3,2,1,0:T(8,128)(2,1)S(1)} collective-permute-done((bf16[1,1,128,768]{3,2,1,0:T(8,128)(2,1)S(1)}, bf16[1,1,128,768]{3,2,1,0:T(8,128)(2,1)S(1)}, u32[]{:S(2)}, u32[]{:S(2)}) %collective-permute-start.5) | collective-permute-done | bytes 196640 | tf_op jit(solution)/shard_map/ppermute | solution.py:71
  76.9 2.2 %collective-permute-start.10 = (bf16[1,1,128,768]{3,2,1,0:T(8,128)(2,1)S(1)}, bf16[1,1,128,768]{3,2,1,0:T(8,128)(2,1)S(1)}, u32[]{:S(2)}, u32[]{:S(2)}) collective-permute-start(bf16[1,1,128,768]{3,2,1,0:T(8,128)(2,1)S(1)} %get-tuple-element.89), channel_id=1, source_target_pairs={{0,11},{1,12},{2,13},{3,14},{4,15},{5,0},{6,1},{7,2},{8,3},{9,4},{... | collective-permute-start | bytes 589832 | tf_op jit(solution)/shard_map/ppermute | solution.py:71
  79.8 5.4 %collective-permute-done.6 = bf16[1,1,128,768]{3,2,1,0:T(8,128)(2,1)S(1)} collective-permute-done((bf16[1,1,128,768]{3,2,1,0:T(8,128)(2,1)S(1)}, bf16[1,1,128,768]{3,2,1,0:T(8,128)(2,1)S(1)}, u32[]{:S(2)}, u32[]{:S(2)}) %collective-permute-start.6) | collective-permute-done | bytes 196640 | tf_op jit(solution)/shard_map/ppermute | solution.py:71
  85.9 3.7 %collective-permute-done.7 = bf16[1,1,128,768]{3,2,1,0:T(8,128)(2,1)S(1)} collective-permute-done((bf16[1,1,128,768]{3,2,1,0:T(8,128)(2,1)S(1)}, bf16[1,1,128,768]{3,2,1,0:T(8,128)(2,1)S(1)}, u32[]{:S(2)}, u32[]{:S(2)}) %collective-permute-start.7) | collective-permute-done | bytes 196640 | tf_op jit(solution)/shard_map/ppermute | solution.py:71
  90.2 2.5 %collective-permute-start.13 = (bf16[1,1,128,768]{3,2,1,0:T(8,128)(2,1)S(1)}, bf16[1,1,128,768]{3,2,1,0:T(8,128)(2,1)S(1)}, u32[]{:S(2)}, u32[]{:S(2)}) collective-permute-start(bf16[1,1,128,768]{3,2,1,0:T(8,128)(2,1)S(1)} %get-tuple-element.86), channel_id=1, source_target_pairs={{0,14},{1,15},{2,0},{3,1},{4,2},{5,3},{6,4},{7,5},{8,6},{9,7},{10,... | collective-permute-start | bytes 589832 | tf_op jit(solution)/shard_map/ppermute | solution.py:71
  100.6 4.3 %gather_fusion.1 = bf16[16,128,768]{2,1,0:T(8,128)(2,1)} fusion(bf16[16,128,768]{2,1,0:T(8,128)(2,1)} %bitcast.44, s32[1024]{0:T(1024)S(1)} %pad_clamp_fusion.1), kind=kCustom, calls=%fused_computation.1 | custom fusion | bytes 6291520 | tf_op jit(solution)/shard_map/gather | solution.py:72
  104.9 4.3 %gather_fusion.2 = bf16[16,128,768]{2,1,0:T(8,128)(2,1)} fusion(bf16[16,128,768]{2,1,0:T(8,128)(2,1)} %gather_fusion.1, s32[1024]{0:T(1024)S(1)} %get-tuple-element.106), kind=kCustom, calls=%fused_computation.2 | custom fusion | bytes 6291520 | tf_op jit(solution)/shard_map/gather | solution.py:74
  109.2 6.2 %convolution_convert_fusion.1 = bf16[2048,768]{1,0:T(8,128)(2,1)} fusion(bf16[2048,768]{1,0:T(8,128)(2,1)} %bitcast.151, bf16[768,768]{1,0:T(8,128)(2,1)S(1)} %copy-done), kind=kOutput, calls=%fused_computation.28 | convolution fusion | flops 2417491968 | bytes 7471104 | tf_op jit(solution)/shard_map/dot_general | solution.py:78
  115.3 4.7 %copy.110 = bf16[2048,768]{0,1:T(8,128)(2,1)} copy(bf16[2048,768]{1,0:T(8,128)(2,1)} %convolution_convert_fusion.1) | data formatting | bytes 6291456 | tf_op jit(solution)/shard_map/convert_element_type | solution.py:78
  120.1 3.0 %copy.126 = bf16[96,8,16,128]{3,2,1,0:T(8,128)(2,1)S(1)} copy(bf16[96,8,16,128]{3,1,2,0:T(8,128)(2,1)} %bitcast.148) | data formatting | bytes 6291456
  123.2 3.9 %convolution_convert_fusion = bf16[2048,768]{1,0:T(8,128)(2,1)} fusion(bf16[2048,768]{1,0:T(8,128)(2,1)S(1)} %bitcast.152, bf16[768,768]{1,0:T(8,128)(2,1)S(1)} %copy-done.7), kind=kOutput, calls=%fused_computation.27 | convolution fusion | flops 2417491968 | bytes 7471104 | tf_op jit(solution)/shard_map/dot_general | solution.py:77
  127.2 4.7 %copy.111 = bf16[2048,768]{0,1:T(8,128)(2,1)} copy(bf16[2048,768]{1,0:T(8,128)(2,1)} %convolution_convert_fusion) | data formatting | bytes 6291456 | tf_op jit(solution)/shard_map/convert_element_type | solution.py:77
  131.9 4.6 %copy.127 = bf16[96,8,16,128]{3,2,1,0:T(8,128)(2,1)} copy(bf16[96,8,16,128]{3,1,2,0:T(8,128)(2,1)} %bitcast.149) | data formatting | bytes 6291456
  136.5 30.5 %while.10 = (s32[]{:T(128)}, bf16[2,128,768]{2,1,0:T(8,128)(2,1)}, s32[2]{0:T(128)S(1)}, bf16[2,8,128,12,64]{2,1,0,4,3:T(8,128)(2,1)S(1)}, bf16[2,8,128,12,64]{2...) while((s32[]{:T(128)}, bf16[2,128,768]{2,1,0:T(8,128)(2,1)}, s32[2]{0:T(128)S(1)}, ...), condition=%wide.region_9.10_spmd, body=%wide.region_5.9_spmd.sunk | while | flops 413761664 | bytes 36668540 | solution.py:101
  140.4 5.9 %fusion.50 = (f32[12,8,128]{2,1,0:T(8,128)S(1)}, f32[12,8,128,128]{2,3,1,0:T(8,128)S(1)}) fusion(f32[12,8,128,128]{3,2,1,0:T(8,128)S(1)} %fusion.49), kind=kOutput, calls=%fused_computation.109.clone.1 | output fusion | flops 6291583 | bytes 12632064 | tf_op jit(solution)/shard_map/while/body/eval_jaxpr/sub | solution.py:91
  155.6 5.9 %fusion.50 = (f32[12,8,128]{2,1,0:T(8,128)S(1)}, f32[12,8,128,128]{2,3,1,0:T(8,128)S(1)}) fusion(f32[12,8,128,128]{3,2,1,0:T(8,128)S(1)} %fusion.49), kind=kOutput, calls=%fused_computation.109.clone.1 | output fusion | flops 6291583 | bytes 12632064 | tf_op jit(solution)/shard_map/while/body/eval_jaxpr/sub | solution.py:91
  167.0 2.8 %fusion.16 = bf16[256,768]{1,0:T(8,128)(2,1)} fusion(bf16[256,768]{1,0:T(8,128)(2,1)} %bitcast.153, bf16[768,768]{1,0:T(8,128)(2,1)} %param.19, bf16[256,768]{1,0:T(8,128)(2,1)} %bitcast.150), kind=kOutput, calls=%fused_computation.31 | convolution fusion | flops 302579712 | bytes 2359296 | tf_op jit(solution)/shard_map/dot_general | solution.py:102
  (103 shorter events, 52.4 us)
Async XLA Ops:
  0.0 109.2 %copy-start = (bf16[768,768]{1,0:T(8,128)(2,1)S(1)}, bf16[768,768]{1,0:T(8,128)(2,1)}, u32[]{:S(2)}) copy-start(bf16[768,768]{1,0:T(8,128)(2,1)} %param.18) | copy-start | bytes 3538948
  4.9 13.5 %all-to-all-start = ((s32[16,1,1]{2,1,0:T(1,128)}), s32[16,1,1]{2,1,0:T(1,128)S(1)}, u32[]{:S(2)}, u32[]{:S(2)}) async-start(s32[16,1,1]{2,1,0:T(1,128)} %copy.95), calls=%async_computation | async-start | bytes 16384 | tf_op jit(solution)/shard_map/all_to_all | solution.py:60
  11.5 6.7 %copy-start.3 = (bf16[2,128,768]{2,1,0:T(8,128)(2,1)S(1)}, bf16[2,128,768]{2,1,0:T(8,128)(2,1)}, u32[]{:S(2)}) copy-start(bf16[2,128,768]{2,1,0:T(8,128)(2,1)} %param.11) | copy-start | bytes 1179652
  11.5 6.7 %copy-start.5 = (f32[768]{0:T(1024)S(1)}, f32[768]{0:T(1024)}, u32[]{:S(2)}) copy-start(f32[768]{0:T(1024)} %param.15) | copy-start | bytes 9220
  21.6 2.8 %copy-start.2 = (bf16[16,128,768]{2,1,0:T(8,128)(2,1)S(1)}, bf16[16,128,768]{2,1,0:T(8,128)(2,1)}, u32[]{:S(2)}) copy-start(bf16[16,128,768]{2,1,0:T(8,128)(2,1)} %gather_fusion) | copy-start | bytes 9437188
  25.0 7.5 %collective-permute-start = (bf16[1,1,128,768]{3,2,1,0:T(8,128)(2,1)S(1)}, bf16[1,1,128,768]{3,2,1,0:T(8,128)(2,1)S(1)}, u32[]{:S(2)}, u32[]{:S(2)}) collective-permute-start(bf16[1,1,128,768]{3,2,1,0:T(8,128)(2,1)S(1)} %get-tuple-element.99), channel_id=1, source_target_pairs={{0,1},{1,2},{2,3},{3,4},{4,5},{5,6},{6,7},{7,8},{8,9},{9,10},{10,1... | collective-permute-start | bytes 589832 | tf_op jit(solution)/shard_map/ppermute | solution.py:71
  26.5 9.8 %collective-permute-start.1 = (bf16[1,1,128,768]{3,2,1,0:T(8,128)(2,1)S(1)}, bf16[1,1,128,768]{3,2,1,0:T(8,128)(2,1)S(1)}, u32[]{:S(2)}, u32[]{:S(2)}) collective-permute-start(bf16[1,1,128,768]{3,2,1,0:T(8,128)(2,1)S(1)} %get-tuple-element.98), channel_id=1, source_target_pairs={{0,2},{1,3},{2,4},{3,5},{4,6},{5,7},{6,8},{7,9},{8,10},{9,11},{10,... | collective-permute-start | bytes 589832 | tf_op jit(solution)/shard_map/ppermute | solution.py:71
  27.7 11.3 %collective-permute-start.2 = (bf16[1,1,128,768]{3,2,1,0:T(8,128)(2,1)S(1)}, bf16[1,1,128,768]{3,2,1,0:T(8,128)(2,1)S(1)}, u32[]{:S(2)}, u32[]{:S(2)}) collective-permute-start(bf16[1,1,128,768]{3,2,1,0:T(8,128)(2,1)S(1)} %get-tuple-element.97), channel_id=1, source_target_pairs={{0,3},{1,4},{2,5},{3,6},{4,7},{5,8},{6,9},{7,10},{8,11},{9,12},{10... | collective-permute-start | bytes 589832 | tf_op jit(solution)/shard_map/ppermute | solution.py:71
  28.1 16.1 %collective-permute-start.3 = (bf16[1,1,128,768]{3,2,1,0:T(8,128)(2,1)S(1)}, bf16[1,1,128,768]{3,2,1,0:T(8,128)(2,1)S(1)}, u32[]{:S(2)}, u32[]{:S(2)}) collective-permute-start(bf16[1,1,128,768]{3,2,1,0:T(8,128)(2,1)S(1)} %get-tuple-element.96), channel_id=1, source_target_pairs={{0,4},{1,5},{2,6},{3,7},{4,8},{5,9},{6,10},{7,11},{8,12},{9,13},{1... | collective-permute-start | bytes 589832 | tf_op jit(solution)/shard_map/ppermute | solution.py:71
  28.9 43.8 %collective-permute-start.4 = (bf16[1,1,128,768]{3,2,1,0:T(8,128)(2,1)S(1)}, bf16[1,1,128,768]{3,2,1,0:T(8,128)(2,1)S(1)}, u32[]{:S(2)}, u32[]{:S(2)}) collective-permute-start(bf16[1,1,128,768]{3,2,1,0:T(8,128)(2,1)S(1)} %get-tuple-element.95), channel_id=1, source_target_pairs={{0,5},{1,6},{2,7},{3,8},{4,9},{5,10},{6,11},{7,12},{8,13},{9,14},{... | collective-permute-start | bytes 589832 | tf_op jit(solution)/shard_map/ppermute | solution.py:71
  32.5 44.4 %collective-permute-start.5 = (bf16[1,1,128,768]{3,2,1,0:T(8,128)(2,1)S(1)}, bf16[1,1,128,768]{3,2,1,0:T(8,128)(2,1)S(1)}, u32[]{:S(2)}, u32[]{:S(2)}) collective-permute-start(bf16[1,1,128,768]{3,2,1,0:T(8,128)(2,1)S(1)} %get-tuple-element.94), channel_id=1, source_target_pairs={{0,6},{1,7},{2,8},{3,9},{4,10},{5,11},{6,12},{7,13},{8,14},{9,15},... | collective-permute-start | bytes 589832 | tf_op jit(solution)/shard_map/ppermute | solution.py:71
  36.3 48.9 %collective-permute-start.6 = (bf16[1,1,128,768]{3,2,1,0:T(8,128)(2,1)S(1)}, bf16[1,1,128,768]{3,2,1,0:T(8,128)(2,1)S(1)}, u32[]{:S(2)}, u32[]{:S(2)}) collective-permute-start(bf16[1,1,128,768]{3,2,1,0:T(8,128)(2,1)S(1)} %get-tuple-element.93), channel_id=1, source_target_pairs={{0,7},{1,8},{2,9},{3,10},{4,11},{5,12},{6,13},{7,14},{8,15},{9,0},... | collective-permute-start | bytes 589832 | tf_op jit(solution)/shard_map/ppermute | solution.py:71
  39.0 50.6 %collective-permute-start.7 = (bf16[1,1,128,768]{3,2,1,0:T(8,128)(2,1)S(1)}, bf16[1,1,128,768]{3,2,1,0:T(8,128)(2,1)S(1)}, u32[]{:S(2)}, u32[]{:S(2)}) collective-permute-start(bf16[1,1,128,768]{3,2,1,0:T(8,128)(2,1)S(1)} %get-tuple-element.92), channel_id=1, source_target_pairs={{0,8},{1,9},{2,10},{3,11},{4,12},{5,13},{6,14},{7,15},{8,0},{9,1},... | collective-permute-start | bytes 589832 | tf_op jit(solution)/shard_map/ppermute | solution.py:71
  44.2 46.0 %collective-permute-start.8 = (bf16[1,1,128,768]{3,2,1,0:T(8,128)(2,1)S(1)}, bf16[1,1,128,768]{3,2,1,0:T(8,128)(2,1)S(1)}, u32[]{:S(2)}, u32[]{:S(2)}) collective-permute-start(bf16[1,1,128,768]{3,2,1,0:T(8,128)(2,1)S(1)} %get-tuple-element.91), channel_id=1, source_target_pairs={{0,9},{1,10},{2,11},{3,12},{4,13},{5,14},{6,15},{7,0},{8,1},{9,2},... | collective-permute-start | bytes 589832 | tf_op jit(solution)/shard_map/ppermute | solution.py:71
  72.7 20.7 %collective-permute-start.9 = (bf16[1,1,128,768]{3,2,1,0:T(8,128)(2,1)S(1)}, bf16[1,1,128,768]{3,2,1,0:T(8,128)(2,1)S(1)}, u32[]{:S(2)}, u32[]{:S(2)}) collective-permute-start(bf16[1,1,128,768]{3,2,1,0:T(8,128)(2,1)S(1)} %get-tuple-element.90), channel_id=1, source_target_pairs={{0,10},{1,11},{2,12},{3,13},{4,14},{5,15},{6,0},{7,1},{8,2},{9,3},... | collective-permute-start | bytes 589832 | tf_op jit(solution)/shard_map/ppermute | solution.py:71
  76.9 17.2 %collective-permute-start.10 = (bf16[1,1,128,768]{3,2,1,0:T(8,128)(2,1)S(1)}, bf16[1,1,128,768]{3,2,1,0:T(8,128)(2,1)S(1)}, u32[]{:S(2)}, u32[]{:S(2)}) collective-permute-start(bf16[1,1,128,768]{3,2,1,0:T(8,128)(2,1)S(1)} %get-tuple-element.89), channel_id=1, source_target_pairs={{0,11},{1,12},{2,13},{3,14},{4,15},{5,0},{6,1},{7,2},{8,3},{9,4},{... | collective-permute-start | bytes 589832 | tf_op jit(solution)/shard_map/ppermute | solution.py:71
  85.2 9.7 %collective-permute-start.11 = (bf16[1,1,128,768]{3,2,1,0:T(8,128)(2,1)S(1)}, bf16[1,1,128,768]{3,2,1,0:T(8,128)(2,1)S(1)}, u32[]{:S(2)}, u32[]{:S(2)}) collective-permute-start(bf16[1,1,128,768]{3,2,1,0:T(8,128)(2,1)S(1)} %get-tuple-element.88), channel_id=1, source_target_pairs={{0,12},{1,13},{2,14},{3,15},{4,0},{5,1},{6,2},{7,3},{8,4},{9,5},{1... | collective-permute-start | bytes 589832 | tf_op jit(solution)/shard_map/ppermute | solution.py:71
  89.5 6.4 %collective-permute-start.12 = (bf16[1,1,128,768]{3,2,1,0:T(8,128)(2,1)S(1)}, bf16[1,1,128,768]{3,2,1,0:T(8,128)(2,1)S(1)}, u32[]{:S(2)}, u32[]{:S(2)}) collective-permute-start(bf16[1,1,128,768]{3,2,1,0:T(8,128)(2,1)S(1)} %get-tuple-element.87), channel_id=1, source_target_pairs={{0,13},{1,14},{2,15},{3,0},{4,1},{5,2},{6,3},{7,4},{8,5},{9,6},{10... | collective-permute-start | bytes 589832 | tf_op jit(solution)/shard_map/ppermute | solution.py:71
  90.2 7.3 %collective-permute-start.13 = (bf16[1,1,128,768]{3,2,1,0:T(8,128)(2,1)S(1)}, bf16[1,1,128,768]{3,2,1,0:T(8,128)(2,1)S(1)}, u32[]{:S(2)}, u32[]{:S(2)}) collective-permute-start(bf16[1,1,128,768]{3,2,1,0:T(8,128)(2,1)S(1)} %get-tuple-element.86), channel_id=1, source_target_pairs={{0,14},{1,15},{2,0},{3,1},{4,2},{5,3},{6,4},{7,5},{8,6},{9,7},{10,... | collective-permute-start | bytes 589832 | tf_op jit(solution)/shard_map/ppermute | solution.py:71
  93.4 6.4 %collective-permute-start.14 = (bf16[1,1,128,768]{3,2,0,1:T(8,128)(2,1)S(1)}, bf16[1,1,128,768]{3,2,0,1:T(8,128)(2,1)S(1)}, u32[]{:S(2)}, u32[]{:S(2)}) collective-permute-start(bf16[1,1,128,768]{3,2,0,1:T(8,128)(2,1)S(1)} %constant_dynamic-slice_fusion.2), channel_id=1, source_target_pairs={{0,15},{1,0},{2,1},{3,2},{4,3},{5,4},{6,5},{7,6},{8,7},{9,8},{10,9... | collective-permute-start | bytes 589832 | tf_op jit(solution)/shard_map/ppermute | solution.py:71
  120.1 3.0 %copy-start.4 = (bf16[16,128,768]{2,1,0:T(8,128)(2,1)S(1)}, bf16[16,128,768]{2,1,0:T(8,128)(2,1)}, u32[]{:S(2)}) copy-start(bf16[16,128,768]{2,1,0:T(8,128)(2,1)} %gather_fusion.2) | copy-start | bytes 9437188
  120.1 3.2 %copy-start.7 = (bf16[768,768]{1,0:T(8,128)(2,1)S(1)}, bf16[768,768]{1,0:T(8,128)(2,1)}, u32[]{:S(2)}) copy-start(bf16[768,768]{1,0:T(8,128)(2,1)} %param.17) | copy-start | bytes 3538948
  131.9 4.6 %copy-start.6 = (s32[2]{0:T(128)S(1)}, s32[2]{0:T(128)}, u32[]{:S(2)}) copy-start(s32[2]{0:T(128)} %param.13) | copy-start | bytes 28
  167.0 2.8 %copy-start.1 = (bf16[768,768]{1,0:T(8,128)(2,1)S(1)}, bf16[768,768]{1,0:T(8,128)(2,1)}, u32[]{:S(2)}) copy-start(bf16[768,768]{1,0:T(8,128)(2,1)} %param.18) | copy-start | bytes 3538948
